TPU v7x, 32 devices: a whole 2x2x4 slice. The times are simulated.
32 devices in a mesh: items: 8 (over z, x), frame: 4 (over y, core).
Axes of the slice: x: 2, y: 2, z: 4, core: 2. Of those that a mesh axis runs over, the one named last changes fastest.
Arguments:
- tokens: bfloat16 [6400, 768], P(('items', 'frame')), may hold values from -6 to 6
- visible_place: int32 [32, 200], P(('items', 'frame')), may hold values from 0 to 799, as said below
- item_index: int32 [32, 800], P(('items', 'frame')), may hold values from 0 to 2, as said below
- out_cotangent: bfloat16 [25600, 512], P(('items', 'frame')), may hold values from -6 to 6
- encoder_norm_gain: float32 [768], replicated, may hold values from 0.1 to 1.9
- encoder_norm_shift: float32 [768], replicated, may hold values from -1.75 to 1.75
- encoder_inward: bfloat16 [768, 2304], replicated, may hold values from -0.3125 to 0.3125
- encoder_query_bias: float32 [768], replicated, may hold values from -1.75 to 1.75
- encoder_value_bias: float32 [768], replicated, may hold values from -1.75 to 1.75
- encoder_outward: bfloat16 [768, 768], replicated, may hold values from -0.875 to 0.875
- encoder_outward_bias: float32 [768], replicated, may hold values from -1.75 to 1.75
- encoder_second_gain: float32 [768], replicated, may hold values from 0.1 to 1.9
- encoder_second_shift: float32 [768], replicated, may hold values from -1.75 to 1.75
- encoder_expand: bfloat16 [768, 3072], replicated, may hold values from -0.21875 to 0.21875
- encoder_expand_bias: float32 [3072], replicated, may hold values from -1.75 to 1.75
- encoder_contract: bfloat16 [3072, 768], replicated, may hold values from -0.109375 to 0.109375
- encoder_contract_bias: float32 [768], replicated, may hold values from -1.75 to 1.75
- embed_weight: bfloat16 [768, 512], replicated, may hold values from -0.21875 to 0.21875
- embed_bias: float32 [512], replicated, may hold values from -1.75 to 1.75
- mask_token: float32 [512], replicated, may hold values from -6 to 6
- decoder_norm_gain: float32 [512], replicated, may hold values from 0.1 to 1.9
- decoder_norm_shift: float32 [512], replicated, may hold values from -1.75 to 1.75
- decoder_inward: bfloat16 [512, 1536], replicated, may hold values from -0.375 to 0.375
- decoder_query_bias: float32 [512], replicated, may hold values from -1.75 to 1.75
- decoder_value_bias: float32 [512], replicated, may hold values from -1.75 to 1.75
- decoder_outward: bfloat16 [512, 512], replicated, may hold values from -1 to 1
- decoder_outward_bias: float32 [512], replicated, may hold values from -1.75 to 1.75
- decoder_second_gain: float32 [512], replicated, may hold values from 0.1 to 1.9
- decoder_second_shift: float32 [512], replicated, may hold values from -1.75 to 1.75
- decoder_expand: bfloat16 [512, 2048], replicated, may hold values from -0.25 to 0.25
- decoder_expand_bias: float32 [2048], replicated, may hold values from -1.75 to 1.75
- decoder_contract: bfloat16 [2048, 512], replicated, may hold values from -0.125 to 0.125
- decoder_contract_bias: float32 [512], replicated, may hold values from -1.75 to 1.75
Outputs:
- encoded: bfloat16 [6400, 768], P(('items', 'frame'))
- decoded: bfloat16 [25600, 512], P(('items', 'frame'))
- tokens_grad: float32 [6400, 768], P(('items', 'frame'))
- grad_encoder_norm_gain: float32 [768], P('items')
- grad_encoder_norm_shift: float32 [768], P('items')
- grad_encoder_inward: float32 [768, 2304], P('items', 'frame')
- grad_encoder_query_bias: float32 [768], P('items')
- grad_encoder_value_bias: float32 [768], P('items')
- grad_encoder_outward: float32 [768, 768], P('items', 'frame')
- grad_encoder_outward_bias: float32 [768], P('items')
- grad_encoder_second_gain: float32 [768], P('items')
- grad_encoder_second_shift: float32 [768], P('items')
- grad_encoder_expand: float32 [768, 3072], P('items', 'frame')
- grad_encoder_expand_bias: float32 [3072], P('items')
- grad_encoder_contract: float32 [3072, 768], P('items', 'frame')
- grad_encoder_contract_bias: float32 [768], P('items')
- grad_embed_weight: float32 [768, 512], P('items', 'frame')
- grad_embed_bias: float32 [512], P('items')
- grad_mask_token: float32 [512], P('items')
- grad_decoder_norm_gain: float32 [512], P('items')
- grad_decoder_norm_shift: float32 [512], P('items')
- grad_decoder_inward: float32 [512, 1536], P('items', 'frame')
- grad_decoder_query_bias: float32 [512], P('items')
- grad_decoder_value_bias: float32 [512], P('items')
- grad_decoder_outward: float32 [512, 512], P('items', 'frame')
- grad_decoder_outward_bias: float32 [512], P('items')
- grad_decoder_second_gain: float32 [512], P('items')
- grad_decoder_second_shift: float32 [512], P('items')
- grad_decoder_expand: float32 [512, 2048], P('items', 'frame')
- grad_decoder_expand_bias: float32 [2048], P('items')
- grad_decoder_contract: float32 [2048, 512], P('items', 'frame')
- grad_decoder_contract_bias: float32 [512], P('items')
Inputs may be any that keep to these rules, and one draw needn't show every extreme that they name: `visible_place`: each row lists 200 distinct places in increasing order, 0 and 799 always among them. `item_index`: the 4 rows of a group are equal. Item numbers never fall along a row; the 3 items are runs of 400, 200 and 200 places, in an order drawn for each group.
All inputs are finite; a program needn't handle non-finite values.
Results may differ from a plain program's by a relative error of at most 0.028.
Values may be sent and summed in bfloat16 or wider, within the bound.
A program may use at most 192 MiB of HBM per device.

v0:
```python
import jax
import jax.numpy as jnp
from jax import lax
from jax.sharding import PartitionSpec as P

HEADS_E = 12
HEADS_D = 16
SIDE = 28


EPSILON = 1e-06
NEGATIVE = -1e30


def sincos(count, angles_in):
    half_count = count // 2
    frequency = 10000.0 ** (-jnp.arange(half_count, dtype=jnp.float32) / half_count)
    angles = angles_in[:, None] * frequency[None, :]
    return jnp.concatenate([jnp.sin(angles), jnp.cos(angles)], axis=1)


def placement_code(frame_value, places, model_width):
    first_part = model_width // 4
    other_part = (model_width - first_part) // 2
    frame_col = jnp.zeros(places.shape, jnp.float32) + frame_value
    return jnp.concatenate(
        [
            sincos(first_part, frame_col),
            sincos(other_part, (places // SIDE).astype(jnp.float32)),
            sincos(other_part, (places % SIDE).astype(jnp.float32)),
        ],
        axis=1,
    )


def normalize(values_in, gain, shift):
    average = jnp.mean(values_in, axis=-1, keepdims=True)
    centred = values_in - average
    spread = jnp.mean(centred * centred, axis=-1, keepdims=True)
    return centred * lax.rsqrt(spread + EPSILON) * gain + shift


def join_heads(stacked):
    return stacked.transpose(1, 0, 2).reshape(stacked.shape[1], stacked.shape[0] * stacked.shape[2])


def attention_forward(queries, keys_all, values_all, same_item, head_count, score_scale):
    head_depth = queries.shape[1] // head_count

    def one_head(head_index):
        offset = head_index * head_depth
        query_head = lax.dynamic_slice_in_dim(queries, offset, head_depth, 1)
        key_head = lax.dynamic_slice_in_dim(keys_all, offset, head_depth, 1)
        value_head = lax.dynamic_slice_in_dim(values_all, offset, head_depth, 1)
        scores = (
            jnp.einsum("qd,kd->qk", query_head, key_head, preferred_element_type=jnp.float32)
            * score_scale
        )
        scores = jnp.where(same_item, scores, NEGATIVE)
        largest = jnp.max(scores, axis=1, keepdims=True)
        exponent = jnp.exp(scores - largest)
        totals = jnp.sum(exponent, axis=1, keepdims=True)
        weights = (exponent / totals).astype(jnp.bfloat16)
        result = jnp.einsum("qk,kd->qd", weights, value_head, preferred_element_type=jnp.float32)
        return (result, largest[:, 0] + jnp.log(totals[:, 0]))

    results, log_sums = lax.map(one_head, jnp.arange(head_count, dtype=jnp.int32))
    return (join_heads(results), log_sums)


def attention_backward(
    attended_grad, queries, keys_all, values_all, same_item, log_sums, head_count, score_scale
):
    head_depth = queries.shape[1] // head_count

    def one_head(head_index):
        offset = head_index * head_depth
        query_head = lax.dynamic_slice_in_dim(queries, offset, head_depth, 1)
        key_head = lax.dynamic_slice_in_dim(keys_all, offset, head_depth, 1)
        value_head = lax.dynamic_slice_in_dim(values_all, offset, head_depth, 1)
        grad_head = lax.dynamic_slice_in_dim(attended_grad, offset, head_depth, 1)
        scores = (
            jnp.einsum("qd,kd->qk", query_head, key_head, preferred_element_type=jnp.float32)
            * score_scale
        )
        scores = jnp.where(same_item, scores, NEGATIVE)
        weights = jnp.exp(scores - log_sums[head_index][:, None])
        weights_low = weights.astype(jnp.bfloat16)
        value_grad = jnp.einsum(
            "qk,qd->kd", weights_low, grad_head, preferred_element_type=jnp.float32
        )
        weight_grad = jnp.einsum(
            "qd,kd->qk", grad_head, value_head, preferred_element_type=jnp.float32
        )
        row_dots = jnp.sum(weights * weight_grad, axis=1, keepdims=True)
        score_grad = (weights * (weight_grad - row_dots)).astype(jnp.bfloat16)
        query_grad = (
            jnp.einsum("qk,kd->qd", score_grad, key_head, preferred_element_type=jnp.float32)
            * score_scale
        )
        key_grad = (
            jnp.einsum("qk,qd->kd", score_grad, query_head, preferred_element_type=jnp.float32)
            * score_scale
        )
        return (query_grad, key_grad, value_grad)

    query_grads, key_grads, value_grads = lax.map(one_head, jnp.arange(head_count, dtype=jnp.int32))
    return (join_heads(query_grads), join_heads(key_grads), join_heads(value_grads))


def block_forward(carried, item_ids, params, head_count, is_encoder):
    (
        norm_gain,
        norm_shift,
        inward,
        query_bias,
        value_bias,
        outward,
        outward_bias,
        second_gain,
        second_shift,
        expand,
        expand_bias,
        contract,
        contract_bias,
    ) = params
    model_width = carried.shape[1]
    score_scale = (model_width // head_count) ** (-0.5)
    normed = normalize(carried, norm_gain, norm_shift).astype(jnp.bfloat16)
    projected = jnp.dot(normed, inward, preferred_element_type=jnp.float32)
    queries = (projected[:, :model_width] + query_bias).astype(jnp.bfloat16)
    keys_local = projected[:, model_width : 2 * model_width].astype(jnp.bfloat16)
    values_local = (projected[:, 2 * model_width :] + value_bias).astype(jnp.bfloat16)
    ids_local = item_ids.astype(jnp.bfloat16)
    if is_encoder:
        keys_all, values_all, ids_all = (
            lax.all_gather(keys_local, "frame", axis=0, tiled=True),
            lax.all_gather(values_local, "frame", axis=0, tiled=True),
            lax.all_gather(ids_local, "frame", axis=0, tiled=True),
        )
    else:
        keys_all, values_all, ids_all = (
            lax.all_gather(keys_local, "frame", axis=0, tiled=True),
            lax.all_gather(values_local, "frame", axis=0, tiled=True),
            lax.all_gather(ids_local, "frame", axis=0, tiled=True),
        )
    same_item = ids_local[:, None] == ids_all[None, :]
    attended, log_sums = attention_forward(
        queries, keys_all, values_all, same_item, head_count, score_scale
    )
    attended = attended.astype(jnp.bfloat16)
    mixed_sum = (
        carried + jnp.dot(attended, outward, preferred_element_type=jnp.float32) + outward_bias
    )
    second = normalize(mixed_sum, second_gain, second_shift).astype(jnp.bfloat16)
    hidden = jnp.dot(second, expand, preferred_element_type=jnp.float32) + expand_bias
    activated = jax.nn.gelu(hidden, approximate=False).astype(jnp.bfloat16)
    output = (
        mixed_sum + jnp.dot(activated, contract, preferred_element_type=jnp.float32) + contract_bias
    )
    gathered = (keys_all, values_all, ids_all)
    kept_values = (
        carried,
        normed,
        queries,
        keys_local,
        values_local,
        ids_local,
        gathered,
        attended,
        log_sums,
        mixed_sum,
        second,
        hidden,
        activated,
    )
    return (output, kept_values)


def block_backward(output_grad, kept_values, params, head_count, is_encoder):
    (
        norm_gain,
        norm_shift,
        inward,
        query_bias,
        value_bias,
        outward,
        outward_bias,
        second_gain,
        second_shift,
        expand,
        expand_bias,
        contract,
        contract_bias,
    ) = params
    (
        carried,
        normed,
        queries,
        keys_local,
        values_local,
        ids_local,
        gathered,
        attended,
        log_sums,
        mixed_sum,
        second,
        hidden,
        activated,
    ) = kept_values
    model_width = carried.shape[1]
    score_scale = (model_width // head_count) ** (-0.5)
    keys_all, values_all, ids_all = gathered
    same_item = ids_local[:, None] == ids_all[None, :]
    contract_in = output_grad.astype(jnp.bfloat16)
    grad_contract_bias = jnp.sum(contract_in.astype(jnp.float32), axis=0)
    grad_contract = jnp.einsum(
        "rc,rd->cd", activated, contract_in, preferred_element_type=jnp.float32
    )
    activated_grad = jnp.einsum(
        "rd,cd->rc", contract_in, contract, preferred_element_type=jnp.float32
    )
    _, gelu_back = jax.vjp(lambda inputs: jax.nn.gelu(inputs, approximate=False), hidden)
    hidden_grad = gelu_back(activated_grad)[0].astype(jnp.bfloat16)
    grad_expand_bias = jnp.sum(hidden_grad.astype(jnp.float32), axis=0)
    grad_expand = jnp.einsum("rw,rc->wc", second, hidden_grad, preferred_element_type=jnp.float32)
    second_grad = jnp.einsum("rc,wc->rw", hidden_grad, expand, preferred_element_type=jnp.float32)
    _, second_back = jax.vjp(normalize, mixed_sum, second_gain, second_shift)
    mixed_part, grad_second_gain, grad_second_shift = second_back(second_grad)
    mixed_grad = output_grad + mixed_part
    branch_grad = mixed_grad.astype(jnp.bfloat16)
    grad_outward_bias = jnp.sum(branch_grad.astype(jnp.float32), axis=0)
    grad_outward = jnp.einsum(
        "rw,rd->wd", attended, branch_grad, preferred_element_type=jnp.float32
    )
    attended_grad = jnp.einsum(
        "rd,wd->rw", branch_grad, outward, preferred_element_type=jnp.float32
    ).astype(jnp.bfloat16)
    query_grad, key_part, value_part = attention_backward(
        attended_grad, queries, keys_all, values_all, same_item, log_sums, head_count, score_scale
    )
    if is_encoder:
        key_grad, value_grad = (
            lax.psum_scatter(
                key_part.astype(jnp.bfloat16), "frame", scatter_dimension=0, tiled=True
            ).astype(jnp.float32),
            lax.psum_scatter(
                value_part.astype(jnp.bfloat16), "frame", scatter_dimension=0, tiled=True
            ).astype(jnp.float32),
        )
    else:
        key_grad, value_grad = (
            lax.psum_scatter(
                key_part.astype(jnp.bfloat16), "frame", scatter_dimension=0, tiled=True
            ).astype(jnp.float32),
            lax.psum_scatter(
                value_part.astype(jnp.bfloat16), "frame", scatter_dimension=0, tiled=True
            ).astype(jnp.float32),
        )
    query_low = query_grad.astype(jnp.bfloat16)
    key_low = key_grad.astype(jnp.bfloat16)
    value_low = value_grad.astype(jnp.bfloat16)
    grad_query_bias = jnp.sum(query_low.astype(jnp.float32), axis=0)
    grad_value_bias = jnp.sum(value_low.astype(jnp.float32), axis=0)
    projection_grad = jnp.concatenate([query_low, key_low, value_low], axis=1)
    grad_inward = jnp.einsum(
        "rw,rc->wc", normed, projection_grad, preferred_element_type=jnp.float32
    )
    normed_grad = jnp.einsum(
        "rc,wc->rw", projection_grad, inward, preferred_element_type=jnp.float32
    )
    _, first_back = jax.vjp(normalize, carried, norm_gain, norm_shift)
    carried_part, grad_norm_gain, grad_norm_shift = first_back(normed_grad)
    carried_grad = mixed_grad + carried_part
    grads = (
        grad_norm_gain,
        grad_norm_shift,
        grad_inward,
        grad_query_bias,
        grad_value_bias,
        grad_outward,
        grad_outward_bias,
        grad_second_gain,
        grad_second_shift,
        grad_expand,
        grad_expand_bias,
        grad_contract,
        grad_contract_bias,
    )
    return (carried_grad, grads)


def body(
    tokens,
    visible_place,
    item_index,
    out_cotangent,
    encoder_norm_gain,
    encoder_norm_shift,
    encoder_inward,
    encoder_query_bias,
    encoder_value_bias,
    encoder_outward,
    encoder_outward_bias,
    encoder_second_gain,
    encoder_second_shift,
    encoder_expand,
    encoder_expand_bias,
    encoder_contract,
    encoder_contract_bias,
    embed_weight,
    embed_bias,
    mask_token,
    decoder_norm_gain,
    decoder_norm_shift,
    decoder_inward,
    decoder_query_bias,
    decoder_value_bias,
    decoder_outward,
    decoder_outward_bias,
    decoder_second_gain,
    decoder_second_shift,
    decoder_expand,
    decoder_expand_bias,
    decoder_contract,
    decoder_contract_bias,
):
    encoder_params = (
        encoder_norm_gain,
        encoder_norm_shift,
        encoder_inward,
        encoder_query_bias,
        encoder_value_bias,
        encoder_outward,
        encoder_outward_bias,
        encoder_second_gain,
        encoder_second_shift,
        encoder_expand,
        encoder_expand_bias,
        encoder_contract,
        encoder_contract_bias,
    )
    decoder_params = (
        decoder_norm_gain,
        decoder_norm_shift,
        decoder_inward,
        decoder_query_bias,
        decoder_value_bias,
        decoder_outward,
        decoder_outward_bias,
        decoder_second_gain,
        decoder_second_shift,
        decoder_expand,
        decoder_expand_bias,
        decoder_contract,
        decoder_contract_bias,
    )
    frame_value = lax.axis_index("frame").astype(jnp.float32)
    places = visible_place[0]
    items_row = item_index[0]
    place_count = items_row.shape[0]
    decoder_width = mask_token.shape[0]
    enc_items = items_row[places]
    carried = tokens.astype(jnp.float32) + placement_code(frame_value, places, tokens.shape[1])
    encoder_out, encoder_kept = block_forward(carried, enc_items, encoder_params, HEADS_E, True)
    encoded = encoder_out.astype(jnp.bfloat16)
    embedded = jnp.dot(encoded, embed_weight, preferred_element_type=jnp.float32) + embed_bias
    filled = (
        jnp.broadcast_to(mask_token[None, :], (place_count, decoder_width)).at[places].set(embedded)
    )
    filled = filled + placement_code(
        frame_value, jnp.arange(place_count, dtype=jnp.int32), decoder_width
    )
    decoder_out, decoder_kept = block_forward(filled, items_row, decoder_params, HEADS_D, False)
    filled_grad, decoder_grads = block_backward(
        out_cotangent.astype(jnp.float32), decoder_kept, decoder_params, HEADS_D, False
    )
    visible_flag = jnp.zeros((place_count,), jnp.float32).at[places].set(1.0)
    mask_grad = jnp.sum(filled_grad * (1.0 - visible_flag)[:, None], axis=0)
    embed_in = filled_grad[places].astype(jnp.bfloat16)
    embed_bias_grad = jnp.sum(embed_in.astype(jnp.float32), axis=0)
    embed_weight_grad = jnp.einsum(
        "re,rd->ed", encoded, embed_in, preferred_element_type=jnp.float32
    )
    encoded_grad = jnp.einsum(
        "rd,ed->re", embed_in, embed_weight, preferred_element_type=jnp.float32
    )
    tokens_grad, encoder_grads = block_backward(
        encoded_grad, encoder_kept, encoder_params, HEADS_E, True
    )
    (
        enc_gain_one,
        enc_shift_one,
        enc_inward_grad,
        enc_query_grad,
        enc_value_grad,
        enc_outward_grad,
        enc_outbias_grad,
        enc_gain_two,
        enc_shift_two,
        enc_expand_grad,
        enc_expbias_grad,
        enc_contract_grad,
        enc_conbias_grad,
    ) = encoder_grads
    (
        dec_gain_one,
        dec_shift_one,
        dec_inward_grad,
        dec_query_grad,
        dec_value_grad,
        dec_outward_grad,
        dec_outbias_grad,
        dec_gain_two,
        dec_shift_two,
        dec_expand_grad,
        dec_expbias_grad,
        dec_contract_grad,
        dec_conbias_grad,
    ) = decoder_grads
    summed = (
        lax.psum_scatter(enc_inward_grad, "items", scatter_dimension=0, tiled=True),
        lax.psum_scatter(enc_outward_grad, "items", scatter_dimension=0, tiled=True),
        lax.psum_scatter(enc_expand_grad, "items", scatter_dimension=0, tiled=True),
        lax.psum_scatter(enc_contract_grad, "items", scatter_dimension=0, tiled=True),
        lax.psum_scatter(embed_weight_grad, "items", scatter_dimension=0, tiled=True),
        lax.psum_scatter(dec_inward_grad, "items", scatter_dimension=0, tiled=True),
        lax.psum_scatter(dec_outward_grad, "items", scatter_dimension=0, tiled=True),
        lax.psum_scatter(dec_expand_grad, "items", scatter_dimension=0, tiled=True),
        lax.psum_scatter(dec_contract_grad, "items", scatter_dimension=0, tiled=True),
        lax.psum_scatter(enc_gain_one, "items", scatter_dimension=0, tiled=True),
        lax.psum_scatter(enc_shift_one, "items", scatter_dimension=0, tiled=True),
        lax.psum_scatter(enc_query_grad, "items", scatter_dimension=0, tiled=True),
        lax.psum_scatter(enc_value_grad, "items", scatter_dimension=0, tiled=True),
        lax.psum_scatter(enc_outbias_grad, "items", scatter_dimension=0, tiled=True),
        lax.psum_scatter(enc_gain_two, "items", scatter_dimension=0, tiled=True),
        lax.psum_scatter(enc_shift_two, "items", scatter_dimension=0, tiled=True),
        lax.psum_scatter(enc_expbias_grad, "items", scatter_dimension=0, tiled=True),
        lax.psum_scatter(enc_conbias_grad, "items", scatter_dimension=0, tiled=True),
        lax.psum_scatter(embed_bias_grad, "items", scatter_dimension=0, tiled=True),
        lax.psum_scatter(mask_grad, "items", scatter_dimension=0, tiled=True),
        lax.psum_scatter(dec_gain_one, "items", scatter_dimension=0, tiled=True),
        lax.psum_scatter(dec_shift_one, "items", scatter_dimension=0, tiled=True),
        lax.psum_scatter(dec_query_grad, "items", scatter_dimension=0, tiled=True),
        lax.psum_scatter(dec_value_grad, "items", scatter_dimension=0, tiled=True),
        lax.psum_scatter(dec_outbias_grad, "items", scatter_dimension=0, tiled=True),
        lax.psum_scatter(dec_gain_two, "items", scatter_dimension=0, tiled=True),
        lax.psum_scatter(dec_shift_two, "items", scatter_dimension=0, tiled=True),
        lax.psum_scatter(dec_expbias_grad, "items", scatter_dimension=0, tiled=True),
        lax.psum_scatter(dec_conbias_grad, "items", scatter_dimension=0, tiled=True),
    )
    matrix_out = (
        lax.psum_scatter(
            summed[0].astype(jnp.bfloat16), "frame", scatter_dimension=1, tiled=True
        ).astype(jnp.float32),
        lax.psum_scatter(
            summed[1].astype(jnp.bfloat16), "frame", scatter_dimension=1, tiled=True
        ).astype(jnp.float32),
        lax.psum_scatter(
            summed[2].astype(jnp.bfloat16), "frame", scatter_dimension=1, tiled=True
        ).astype(jnp.float32),
        lax.psum_scatter(
            summed[3].astype(jnp.bfloat16), "frame", scatter_dimension=1, tiled=True
        ).astype(jnp.float32),
        lax.psum_scatter(
            summed[4].astype(jnp.bfloat16), "frame", scatter_dimension=1, tiled=True
        ).astype(jnp.float32),
        lax.psum_scatter(
            summed[5].astype(jnp.bfloat16), "frame", scatter_dimension=1, tiled=True
        ).astype(jnp.float32),
        lax.psum_scatter(
            summed[6].astype(jnp.bfloat16), "frame", scatter_dimension=1, tiled=True
        ).astype(jnp.float32),
        lax.psum_scatter(
            summed[7].astype(jnp.bfloat16), "frame", scatter_dimension=1, tiled=True
        ).astype(jnp.float32),
        lax.psum_scatter(
            summed[8].astype(jnp.bfloat16), "frame", scatter_dimension=1, tiled=True
        ).astype(jnp.float32),
    )
    vector_out = lax.psum(
        (
            summed[9],
            summed[10],
            summed[11],
            summed[12],
            summed[13],
            summed[14],
            summed[15],
            summed[16],
            summed[17],
            summed[18],
            summed[19],
            summed[20],
            summed[21],
            summed[22],
            summed[23],
            summed[24],
            summed[25],
            summed[26],
            summed[27],
            summed[28],
        ),
        "frame",
    )
    encoder_out_grads = (
        vector_out[0],
        vector_out[1],
        matrix_out[0],
        vector_out[2],
        vector_out[3],
        matrix_out[1],
        vector_out[4],
        vector_out[5],
        vector_out[6],
        matrix_out[2],
        vector_out[7],
        matrix_out[3],
        vector_out[8],
    )
    embed_out_grads = (matrix_out[4], vector_out[9], vector_out[10])
    decoder_out_grads = (
        vector_out[11],
        vector_out[12],
        matrix_out[5],
        vector_out[13],
        vector_out[14],
        matrix_out[6],
        vector_out[15],
        vector_out[16],
        vector_out[17],
        matrix_out[7],
        vector_out[18],
        matrix_out[8],
        vector_out[19],
    )
    return (
        encoded,
        decoder_out.astype(jnp.bfloat16),
        tokens_grad,
        *encoder_out_grads,
        *embed_out_grads,
        *decoder_out_grads,
    )


def solution(mesh):
    return jax.shard_map(
        body,
        mesh=mesh,
        in_specs=(
            P(("items", "frame"), None),
            P(("items", "frame"), None),
            P(("items", "frame"), None),
            P(("items", "frame"), None),
            P(),
            P(),
            P(),
            P(),
            P(),
            P(),
            P(),
            P(),
            P(),
            P(),
            P(),
            P(),
            P(),
            P(),
            P(),
            P(),
            P(),
            P(),
            P(),
            P(),
            P(),
            P(),
            P(),
            P(),
            P(),
            P(),
            P(),
            P(),
            P(),
        ),
        out_specs=(
            P(("items", "frame"), None),
            P(("items", "frame"), None),
            P(("items", "frame"), None),
            P("items"),
            P("items"),
            P("items", "frame"),
            P("items"),
            P("items"),
            P("items", "frame"),
            P("items"),
            P("items"),
            P("items"),
            P("items", "frame"),
            P("items"),
            P("items", "frame"),
            P("items"),
            P("items", "frame"),
            P("items"),
            P("items"),
            P("items"),
            P("items"),
            P("items", "frame"),
            P("items"),
            P("items"),
            P("items", "frame"),
            P("items"),
            P("items"),
            P("items"),
            P("items", "frame"),
            P("items"),
            P("items", "frame"),
            P("items"),
        ),
        check_vma=False,
    )
```

profile of v0, /device:TPU:0, one launch (start us, length us, event | category | flops | bytes accessed | tf_op | source)
XLA Modules:
  0.0 2649.4 jit_solution(17824375543735437928)
XLA Ops:
  63.4 82.6 %while.56 = (s32[]{:T(128)}, bf16[12,200,64]{1,2,0:T(8,128)(2,1)}, f32[12,200]{1,0:T(8,128)}, s32[12]{0:T(128)}, bf16[200,768]{1,0:T(8,128)(2,1)}, /*index=5*/bf...) while((s32[]{:T(128)}, bf16[12,200,64]{1,2,0:T(8,128)(2,1)}, ...), condition=%wide.region_5.6_spmd.clone, body=%wide.region_2.5_spmd.clone.sunk | while | flops 42399804 | bytes 2458123 | solution.py:67
  177.7 26.4 all-gather.11.cloned.1.call-done
  204.1 30.7 %all-gather.9.cloned.1.call-done = bf16[3200,512]{1,0:T(8,128)(2,1)} async-done(((bf16[800,512]{1,0:T(8,128)(2,1)}), bf16[3200,512]{1,0:T(8,128)(2,1)}) %all-gather.9.cloned.1.call-update) | async-done | bytes 3276816 | tf_op jit(solution)/shard_map/all_gather | solution.py:143
  236.4 201.4 %while.57 = (s32[]{:T(128)}, bf16[16,800,32]{1,2,0:T(8,128)(2,1)}, f32[16,800]{1,0:T(8,128)}, s32[16]{0:T(128)}, bf16[800,512]{1,0:T(8,128)(2,1)}, /*index=5*/bf...) while((s32[]{:T(128)}, bf16[16,800,32]{1,2,0:T(8,128)(2,1)}, ...), condition=%wide.region_14.15_spmd.clone, body=%wide.region_11.14_spmd.clone.sunk | while | flops 350719200 | bytes 32725516 | solution.py:67
  472.8 622.7 %while.58 = (s32[]{:T(128)}, bf16[16,800,32]{1,2,0:T(8,128)(2,1)}, bf16[16,3200,32]{1,2,0:T(8,128)(2,1)}, bf16[16,3200,32]{1,2,0:T(8,128)(2,1)}, s32[16]{0:T(128...) while((s32[]{:T(128)}, bf16[16,800,32]{1,2,0:T(8,128)(2,1)}, ...), condition=%wide.region_21.22_spmd.clone, body=%wide.region_19.21_spmd.clone.sunk | while | flops 844927232 | bytes 142477648 | solution.py:107
  1108.4 31.8 %reduce-scatter.69.cloned.1.call-done = bf16[800,512]{1,0:T(8,128)(2,1)} async-done(((bf16[3200,512]{1,0:T(8,128)(2,1)}), bf16[800,512]{1,0:T(8,128)(2,1)}) %reduce-scatter.69.cloned.1.call-update) | async-done | bytes 819216
  1142.5 39.0 %reduce-scatter.67.cloned.1.call-done = bf16[800,512]{1,0:T(8,128)(2,1)} async-done(((bf16[3200,512]{1,0:T(8,128)(2,1)}), bf16[800,512]{1,0:T(8,128)(2,1)}) %reduce-scatter.67.cloned.1.call-update) | async-done | bytes 819216
  1210.3 148.4 %while.59 = (s32[]{:T(128)}, bf16[12,200,64]{1,2,0:T(8,128)(2,1)}, bf16[12,800,64]{1,2,0:T(8,128)(2,1)}, bf16[12,800,64]{1,2,0:T(8,128)(2,1)}, s32[12]{0:T(128)S...) while((s32[]{:T(128)}, bf16[12,200,64]{1,2,0:T(8,128)(2,1)}, ...), condition=%wide.region_30.31_spmd.clone, body=%wide.region_28.30_spmd.clone.sunk | while | flops 104063808 | bytes 6152381 | solution.py:107
  1395.8 20.4 reduce-scatter.71.cloned.1.call-done
  1437.8 45.3 %reduce-scatter.59.cloned.1.call-done = f32[64,512]{1,0:T(8,128)} async-done(((f32[512,512]{1,0:T(8,128)}), f32[64,512]{1,0:T(8,128)}) %reduce-scatter.59.cloned.1.call-update) | async-done | bytes 131088 | tf_op jit(solution)/shard_map/reduce_scatter | solution.py:428
  1486.4 87.5 %reduce-scatter.65.cloned.1.call-done = f32[256,512]{1,0:T(8,128)} async-done(((f32[2048,512]{1,0:T(8,128)}), f32[256,512]{1,0:T(8,128)}) %reduce-scatter.65.cloned.1.call-update) | async-done | bytes 524304 | tf_op jit(solution)/shard_map/reduce_scatter | solution.py:430
  1585.0 80.3 %reduce-scatter.61.cloned.1.call-done = f32[64,2048]{1,0:T(8,128)} async-done(((f32[512,2048]{1,0:T(8,128)}), f32[64,2048]{1,0:T(8,128)}) %reduce-scatter.61.cloned.1.call-update) | async-done | bytes 524304 | tf_op jit(solution)/shard_map/reduce_scatter | solution.py:429
  1673.7 59.9 %reduce-scatter.55.cloned.1.call-done = f32[96,512]{1,0:T(8,128)} async-done(((f32[768,512]{1,0:T(8,128)}), f32[96,512]{1,0:T(8,128)}) %reduce-scatter.55.cloned.1.call-update) | async-done | bytes 196624 | tf_op jit(solution)/shard_map/reduce_scatter | solution.py:426
  1736.9 68.2 %reduce-scatter.47.cloned.1.call-done = f32[96,768]{1,0:T(8,128)} async-done(((f32[768,768]{1,0:T(8,128)}), f32[96,768]{1,0:T(8,128)}) %reduce-scatter.47.cloned.1.call-update) | async-done | bytes 294928 | tf_op jit(solution)/shard_map/reduce_scatter | solution.py:423
  1808.5 73.6 %reduce-scatter.57.cloned.1.call-done = f32[64,1536]{1,0:T(8,128)} async-done(((f32[512,1536]{1,0:T(8,128)}), f32[64,1536]{1,0:T(8,128)}) %reduce-scatter.57.cloned.1.call-update) | async-done | bytes 393232 | tf_op jit(solution)/shard_map/reduce_scatter | solution.py:427
  1885.7 128.1 %reduce-scatter.45.cloned.1.call-done = f32[96,2304]{1,0:T(8,128)} async-done(((f32[768,2304]{1,0:T(8,128)}), f32[96,2304]{1,0:T(8,128)}) %reduce-scatter.45.cloned.1.call-update) | async-done | bytes 884752 | tf_op jit(solution)/shard_map/reduce_scatter | solution.py:422
  2017.9 162.3 %reduce-scatter.53.cloned.1.call-done = f32[384,768]{1,0:T(8,128)} async-done(((f32[3072,768]{1,0:T(8,128)}), f32[384,768]{1,0:T(8,128)}) %reduce-scatter.53.cloned.1.call-update) | async-done | bytes 1179664 | tf_op jit(solution)/shard_map/reduce_scatter | solution.py:425
  2184.6 162.1 %reduce-scatter.49.cloned.1.call-done = f32[96,3072]{1,0:T(8,128)} async-done(((f32[768,3072]{1,0:T(8,128)}), f32[96,3072]{1,0:T(8,128)}) %reduce-scatter.49.cloned.1.call-update) | async-done | bytes 1179664 | tf_op jit(solution)/shard_map/reduce_scatter | solution.py:424
  2369.8 21.6 reduce-scatter.87.cloned.1.call-done
  2416.0 82.4 %all-reduce.27.cloned.1.call-done = (f32[768]{0:T(1024)}, f32[768]{0:T(1024)}, f32[768]{0:T(1024)}, f32[768]{0:T(1024)}, f32[768]{0:T(1024)}, /*index=5*/f32[768...) async-done(((f32[768]{0:T(1024)}, f32[768]{0:T(1024)}, ...) | async-done | bytes 65552
  2546.3 20.4 reduce-scatter.83.cloned.1.call-done
  2569.8 21.7 reduce-scatter.75.cloned.1.call-done
  2594.8 21.3 reduce-scatter.79.cloned.1.call-done
  2619.6 21.1 reduce-scatter.51.cloned.1.call-done
  (969 shorter events, 1333.5 us)
Async XLA Ops:
  24.1 180.0 %all-gather.11.cloned.1.call-start = ((), (), s32[]{:S(2)}) async-start(), calls=%async_computation.25 | async-start | bytes 4096000 | tf_op jit(solution)/shard_map/all_gather | solution.py:144
  174.6 60.2 %all-gather.9.cloned.1.call-start = ((), (), s32[]{:S(2)}) async-start(), calls=%async_computation.24 | async-start | bytes 4096000 | tf_op jit(solution)/shard_map/all_gather | solution.py:143
  177.2 962.9 %reduce-scatter.69.cloned.1.call-start = ((), (), s32[]{:S(2)}) async-start(), calls=%async_computation.38 | async-start | bytes 4096000
  1101.2 80.3 %reduce-scatter.67.cloned.1.call-start = ((), (), s32[]{:S(2)}) async-start(), calls=%async_computation.37 | async-start | bytes 4096000
  1106.9 287.0 %reduce-scatter.73.cloned.1.call-start = ((), (), s32[]{:S(2)}) async-start(), calls=%async_computation.40 | async-start | bytes 1536000
  1363.8 119.3 %reduce-scatter.59.cloned.1.call-start = ((), (), s32[]{:S(2)}) async-start(), calls=%async_computation.33 | async-start | bytes 1179648 | tf_op jit(solution)/shard_map/reduce_scatter | solution.py:428
  1367.0 207.0 %reduce-scatter.65.cloned.1.call-start = ((), (), s32[]{:S(2)}) async-start(), calls=%async_computation.36 | async-start | bytes 4718592 | tf_op jit(solution)/shard_map/reduce_scatter | solution.py:430
  1374.2 291.1 %reduce-scatter.61.cloned.1.call-start = ((), (), s32[]{:S(2)}) async-start(), calls=%async_computation.34 | async-start | bytes 4718592 | tf_op jit(solution)/shard_map/reduce_scatter | solution.py:429
  1381.8 351.8 %reduce-scatter.55.cloned.1.call-start = ((), (), s32[]{:S(2)}) async-start(), calls=%async_computation.31 | async-start | bytes 1769472 | tf_op jit(solution)/shard_map/reduce_scatter | solution.py:426
  1384.5 420.5 %reduce-scatter.47.cloned.1.call-start = ((), (), s32[]{:S(2)}) async-start(), calls=%async_computation.27 | async-start | bytes 2654208 | tf_op jit(solution)/shard_map/reduce_scatter | solution.py:423
  1387.6 494.4 %reduce-scatter.57.cloned.1.call-start = ((), (), s32[]{:S(2)}) async-start(), calls=%async_computation.32 | async-start | bytes 3538944 | tf_op jit(solution)/shard_map/reduce_scatter | solution.py:427
  1393.8 619.9 %reduce-scatter.45.cloned.1.call-start = ((), (), s32[]{:S(2)}) async-start(), calls=%async_computation.26 | async-start | bytes 7962624 | tf_op jit(solution)/shard_map/reduce_scatter | solution.py:422
  1423.8 756.4 %reduce-scatter.53.cloned.1.call-start = ((), (), s32[]{:S(2)}) async-start(), calls=%async_computation.30 | async-start | bytes 10616832 | tf_op jit(solution)/shard_map/reduce_scatter | solution.py:425
  1430.3 916.3 %reduce-scatter.49.cloned.1.call-start = ((), (), s32[]{:S(2)}) async-start(), calls=%async_computation.28 | async-start | bytes 10616832 | tf_op jit(solution)/shard_map/reduce_scatter | solution.py:424
  1437.7 930.6 %reduce-scatter.85.cloned.1.call-start = ((), (), s32[]{:S(2)}) async-start(), calls=%async_computation.46 | async-start | bytes 163840
  1486.2 905.2 %reduce-scatter.87.cloned.1.call-start = ((), (), s32[]{:S(2)}) async-start(), calls=%async_computation.47 | async-start | bytes 327680
  1577.5 837.0 %reduce-scatter.63.cloned.1.call-start = ((), (), s32[]{:S(2)}) async-start(), calls=%async_computation.35 | async-start | bytes 327680 | tf_op jit(solution)/shard_map/reduce_scatter | solution.py:474
  1667.1 831.3 %all-reduce.27.cloned.1.call-start = ((), (), s32[]{:S(2)}) async-start(), calls=%async_computation.48 | async-start | bytes 147456
  1673.7 859.2 %reduce-scatter.81.cloned.1.call-start = ((), (), s32[]{:S(2)}) async-start(), calls=%async_computation.44 | async-start | bytes 163840
  1736.8 806.6 %reduce-scatter.77.cloned.1.call-start = ((), (), s32[]{:S(2)}) async-start(), calls=%async_computation.42 | async-start | bytes 245760
  1808.4 758.3 %reduce-scatter.83.cloned.1.call-start = ((), (), s32[]{:S(2)}) async-start(), calls=%async_computation.45 | async-start | bytes 491520
  1885.6 705.9 %reduce-scatter.75.cloned.1.call-start = ((), (), s32[]{:S(2)}) async-start(), calls=%async_computation.41 | async-start | bytes 737280
  2017.8 598.3 %reduce-scatter.79.cloned.1.call-start = ((), (), s32[]{:S(2)}) async-start(), calls=%async_computation.43 | async-start | bytes 737280
  2184.5 456.2 %reduce-scatter.51.cloned.1.call-start = ((), (), s32[]{:S(2)}) async-start(), calls=%async_computation.29 | async-start | bytes 737280 | tf_op jit(solution)/shard_map/reduce_scatter | solution.py:459
  (163 other events, 1486.3 us)
Sparse Core Ops, SparseCore 0:
  22.3 20.4 all-gather.6
  174.7 29.2 all-gather.10
  205.5 29.2 all-gather.8
  1101.3 38.7 reduce-scatter.68
  1142.7 38.7 reduce-scatter.66
  1361.3 26.0 reduce-scatter.72
  1390.1 26.0 reduce-scatter.70
  1419.6 63.3 reduce-scatter.58
  1487.0 86.9 reduce-scatter.64
  1577.6 87.6 reduce-scatter.60
  1668.9 64.5 reduce-scatter.54
  1737.1 67.9 reduce-scatter.46
  1808.5 73.5 reduce-scatter.56
  1885.6 128.0 reduce-scatter.44
  2017.6 162.5 reduce-scatter.52
  2184.1 162.5 reduce-scatter.48
  2371.4 20.0 reduce-scatter.86
  2394.5 19.9 reduce-scatter.62
  2421.7 76.7 all-reduce.26
  2523.6 19.7 reduce-scatter.76
  2545.9 20.8 reduce-scatter.82
  2569.4 22.0 reduce-scatter.74
  2594.0 22.0 reduce-scatter.78
  2618.6 22.0 reduce-scatter.50
  (3 shorter events, 55.8 us)
where the time goes:
time: 2670 us; the launch traced here: 2650 us
  waiting for transfers between devices  1250 us (47%)
  matrix products  775 us (29%)
  other arithmetic  261 us (10%)
  local copies, waits for them, and re-layouts  222 us (8%)
  loops' own time  92 us (3%)
    unnamed x39, waiting for transfers between devices  277 us
    dot_general x56, matrix products, one_head(): jnp.einsum('qd,kd->qk', query_head, key_head, preferred_element_type=jnp....  252 us
    convert_element_type x28, other arithmetic, one_head(): score_grad = (weights * (weight_grad - row_dots)).astype(jnp.bfloat16)  172 us
    reduce_scatter x1, waiting for transfers between devices, body(): lax.psum_scatter(enc_contract_grad, 'items', scatter_dimension=0, tiled=T...  162 us
    reduce_scatter x1, waiting for transfers between devices, body(): lax.psum_scatter(enc_expand_grad, 'items', scatter_dimension=0, tiled=True)  162 us
    reduce_scatter x1, waiting for transfers between devices, body(): lax.psum_scatter(enc_inward_grad, 'items', scatter_dimension=0, tiled=True)  128 us
    dot_general x28, matrix products, one_head(): jnp.einsum('qk,qd->kd', weights_low, grad_head, preferred_element_type=jn...  114 us
    reduce_scatter x1, waiting for transfers between devices, body(): lax.psum_scatter(dec_contract_grad, 'items', scatter_dimension=0, tiled=T...  87.5 us
  transfers between devices with their start and end apart: 27, of which 24 were waited for; matrix products, arithmetic and copies ran while one was open for 7% of the time, Pallas kernels for 0%

commit v1 on v0

v1 whole, which is shorter than its diff:
```python
import functools

import numpy as np
import jax
import jax.numpy as jnp
from jax import lax
from jax.experimental import pallas as pl
from jax.experimental.pallas import tpu as pltpu
from jax.sharding import PartitionSpec as P

HEADS_E = 12
HEADS_D = 16
SIDE = 28
EPSILON = 1e-06
MESH = pl.DeviceIdType.MESH

LOG2E = 1.4426950408889634
NEG = -1e30
LANE = 128
def dot_nt(a, b):
    return lax.dot_general(a, b, (((1,), (1,)), ((), ())), preferred_element_type=jnp.float32)
def dot_nn(a, b):
    return lax.dot_general(a, b, (((1,), (0,)), ((), ())), preferred_element_type=jnp.float32)
def head_parts(x, depth):
    per = LANE // depth
    lane = lax.broadcasted_iota(jnp.int32, x.shape, 1) // depth
    return [jnp.where(lane == h, x, jnp.zeros_like(x)) for h in range(per)]

def fwd_kernel(depth, segs, kc, masked, *refs):
    if masked:
        q_ref, k_ref, v_ref, idq_ref, idk_ref, o_ref, lse_ref = refs
    else:
        q_ref, k_ref, v_ref, o_ref, lse_ref = refs
    per = LANE // depth
    coef = depth ** -0.5 * LOG2E
    for g, (q0, qn, k0, kn) in enumerate(segs):
        qm = head_parts(q_ref[q0:q0 + qn, :], depth)
        step = kc if kn % kc == 0 else kn
        def chunk(c, carry):
            ms, ls, accs = carry
            rows = pl.ds(pl.multiple_of(k0 + c * step, 16), step)
            kk = k_ref[rows, :]
            vt = v_ref[rows, :].T
            if masked:
                same = idk_ref[rows, :1] == idq_ref[:1, :qn]
            nm, nl, na = [], [], []
            for h in range(per):
                s = dot_nt(kk, qm[h])
                if masked:
                    s = jnp.where(same, s, NEG)
                m = jnp.maximum(ms[h], jnp.max(s, axis=0, keepdims=True) * coef)
                alpha = jnp.exp2(ms[h] - m)
                p = jnp.exp2(s * coef - m)
                nl.append(ls[h] * alpha + jnp.sum(p, axis=0, keepdims=True))
                na.append(accs[h] * alpha + dot_nn(vt[h * depth:(h + 1) * depth], p.astype(jnp.bfloat16)))
                nm.append(m)
            return nm, nl, na
        init = ([jnp.full((1, qn), NEG * coef, jnp.float32)] * per, [jnp.zeros((1, qn), jnp.float32)] * per, [jnp.zeros((depth, qn), jnp.float32)] * per)
        if kn == step:
            ms, ls, accs = chunk(0, init)
        else:
            ms, ls, accs = lax.fori_loop(0, kn // step, chunk, init)
        out = jnp.concatenate([accs[h] / ls[h] for h in range(per)], axis=0)
        o_ref[q0:q0 + qn, :] = out.T.astype(o_ref.dtype)
        for h in range(per):
            lse_ref[0, g, h:h + 1, :qn] = ms[h] + jnp.log2(ls[h])

def attn_fwd(q, k, v, depth, segs, kc, ids=None):
    rows, n = q.shape; keys = k.shape[0]; tiles = n // LANE
    qpad = max(-(-s[1] // LANE) * LANE for s in segs)
    col = lambda r: pl.BlockSpec((r, LANE), lambda t: (0, t))
    ins = [q, k, v]; specs = [col(rows), col(keys), col(keys)]
    if ids is not None:
        ins += list(ids); specs += [pl.BlockSpec(i.shape, lambda t: (0, 0)) for i in ids]
    per = LANE // depth
    pairs = sum(s[1] * s[3] for s in segs)
    return pl.pallas_call(
        functools.partial(fwd_kernel, depth, segs, kc, ids is not None),
        grid=(tiles,), in_specs=specs,
        out_specs=[col(rows), pl.BlockSpec((1, len(segs), 8, qpad), lambda t: (t, 0, 0, 0))],
        out_shape=[jax.ShapeDtypeStruct((rows, n), jnp.bfloat16), jax.ShapeDtypeStruct((tiles, len(segs), 8, qpad), jnp.float32)],
        compiler_params=pltpu.CompilerParams(vmem_limit_bytes=48 << 20),
        cost_estimate=pl.CostEstimate(flops=4 * pairs * n, bytes_accessed=2 * n * (2 * rows + 2 * keys), transcendentals=pairs * n // depth),
        name="attention_forward",
    )(*ins)

def bwd_kernel(depth, segs, kc, masked, *refs):
    if masked:
        q_ref, k_ref, v_ref, do_ref, o_ref, lse_ref, idq_ref, idk_ref, dq_ref, dk_ref, dv_ref = refs
    else:
        q_ref, k_ref, v_ref, do_ref, o_ref, lse_ref, dq_ref, dk_ref, dv_ref = refs
    per = LANE // depth
    scale = depth ** -0.5
    coef = scale * LOG2E
    pick = (lax.broadcasted_iota(jnp.int32, (8, LANE), 1) // depth == lax.broadcasted_iota(jnp.int32, (8, LANE), 0)).astype(jnp.float32)
    for g, (q0, qn, k0, kn) in enumerate(segs):
        do = do_ref[q0:q0 + qn, :]
        qm = head_parts(q_ref[q0:q0 + qn, :], depth)
        dom = head_parts(do, depth)
        delta = lax.dot_general(pick, do.astype(jnp.float32) * o_ref[q0:q0 + qn, :].astype(jnp.float32), (((1,), (1,)), ((), ())), preferred_element_type=jnp.float32, precision=lax.Precision.HIGHEST)
        step = kc if kn % kc == 0 else kn
        def chunk(c, carry):
            rows = pl.ds(pl.multiple_of(k0 + c * step, 16), step)
            kk = k_ref[rows, :]
            vv = v_ref[rows, :]
            kt = kk.T
            if masked:
                same = idk_ref[rows, :1] == idq_ref[:1, :qn]
            dv = jnp.zeros((step, LANE), jnp.float32)
            dk = jnp.zeros((step, LANE), jnp.float32)
            new = []
            for h in range(per):
                s = dot_nt(kk, qm[h])
                if masked:
                    s = jnp.where(same, s, NEG)
                p = jnp.exp2(s * coef - lse_ref[0, g, h:h + 1, :qn])
                dp = dot_nt(vv, dom[h])
                dv = dv + dot_nn(p.astype(jnp.bfloat16), dom[h])
                ds = (p * (dp - delta[h:h + 1, :])).astype(jnp.bfloat16)
                dk = dk + dot_nn(ds, qm[h])
                new.append(carry[h] + dot_nn(kt[h * depth:(h + 1) * depth], ds))
            dk_ref[rows, :] = (dk * scale).astype(dk_ref.dtype)
            dv_ref[rows, :] = dv.astype(dv_ref.dtype)
            return new
        init = [jnp.zeros((depth, qn), jnp.float32)] * per
        if kn == step:
            dqs = chunk(0, init)
        else:
            dqs = lax.fori_loop(0, kn // step, chunk, init)
        dq_ref[q0:q0 + qn, :] = (jnp.concatenate(dqs, axis=0).T * scale).astype(dq_ref.dtype)

def attn_bwd(q, k, v, do, o, lse, depth, segs, kc, ids=None):
    rows, n = q.shape; keys = k.shape[0]; tiles = n // LANE
    col = lambda r: pl.BlockSpec((r, LANE), lambda t: (0, t))
    ins = [q, k, v, do, o, lse]
    specs = [col(rows), col(keys), col(keys), col(rows), col(rows), pl.BlockSpec((1,) + lse.shape[1:], lambda t: (t, 0, 0, 0))]
    if ids is not None:
        ins += list(ids); specs += [pl.BlockSpec(i.shape, lambda t: (0, 0)) for i in ids]
    pairs = sum(s[1] * s[3] for s in segs)
    return pl.pallas_call(
        functools.partial(bwd_kernel, depth, segs, kc, ids is not None),
        grid=(tiles,), in_specs=specs,
        out_specs=[col(rows), col(keys), col(keys)],
        out_shape=[jax.ShapeDtypeStruct((rows, n), jnp.bfloat16), jax.ShapeDtypeStruct((keys, n), jnp.bfloat16), jax.ShapeDtypeStruct((keys, n), jnp.bfloat16)],
        compiler_params=pltpu.CompilerParams(vmem_limit_bytes=48 << 20),
        cost_estimate=pl.CostEstimate(flops=10 * pairs * n, bytes_accessed=2 * n * (4 * rows + 4 * keys), transcendentals=pairs * n // depth),
        name="attention_backward",
    )(*ins)


def bits_of(count):
    return count.bit_length() - 1


class Plan:
    def __init__(self, n_items, n_frame):
        self.n_items, self.n_frame = n_items, n_frame
        self.digits = [("frame", 1 << b) for b in reversed(range(bits_of(n_frame)))]
        self.digits += [("items", 1 << b) for b in reversed(range(bits_of(n_items)))]

    def mine(self, d):
        axis, weight = self.digits[d]
        return lax.rem(lax.div(lax.axis_index(axis), weight), 2)

    def partner(self, d):
        axis, weight = self.digits[d]
        item, frame = lax.axis_index("items"), lax.axis_index("frame")
        step = weight * (1 - 2 * self.mine(d))
        return (item + step, frame) if axis == "items" else (item, frame + step)


def wgrad_kernel(plan, units, n_vec, *refs):
    nu = len(units)
    nd = len(plan.digits)
    core = bits_of(plan.n_frame) - 1
    pos = 0
    a_refs, b_refs = refs[0:2 * nu:2], refs[1:2 * nu:2]
    pos = 2 * nu
    if n_vec:
        vec_ref = refs[pos]
        pos += 1
    out_refs = refs[pos:pos + nu]
    pos += nu
    if n_vec:
        vec_out = refs[pos]
        pos += 1
    send0, acc0 = refs[pos:pos + nu], refs[pos + nu:pos + 2 * nu]
    pos += 2 * nu
    recv = [refs[pos + u * nd:pos + (u + 1) * nd] for u in range(nu)]
    pos += nu * nd
    if n_vec:
        vsum, vrecv = refs[pos], refs[pos + 1]
        pos += 2
    send_sem, recv_sem = refs[pos], refs[pos + 1]

    barrier = pltpu.get_barrier_semaphore()
    for d in range(nd):
        pl.semaphore_signal(barrier, inc=1, device_id=plan.partner(d), device_id_type=MESH)

    half = plan.n_frame // 2

    def blocks(u, mine, dst):
        transposed = units[u]["t"]

        def one(c, carry):
            f = 2 * c + mine
            if transposed:
                g = dot_nn(b_refs[u][f].T, a_refs[u][...])
            else:
                g = lax.dot_general(a_refs[u][...], b_refs[u][f], (((0,), (0,)), ((), ())), preferred_element_type=jnp.float32)
            size = g.shape[1 if transposed else 0] // plan.n_items
            for i in range(plan.n_items):
                part = g[:, i * size:(i + 1) * size] if transposed else g[i * size:(i + 1) * size]
                index = tuple((i >> b) & 1 for b in reversed(range(bits_of(plan.n_items))))
                dst[(c,) + index] = part.astype(jnp.bfloat16)
            return carry

        lax.fori_loop(0, half, one, 0)

    copies = []

    def send(u, step, src, dst, digit):
        copy = pltpu.make_async_remote_copy(
            src_ref=src, dst_ref=dst, send_sem=send_sem.at[u, step], recv_sem=recv_sem.at[u, step],
            device_id=plan.partner(digit), device_id_type=MESH)
        copy.start()
        copies.append(copy)
        return copy

    orders = [[core] + list(unit["order"]) for unit in units]
    flight = {}
    state = {}

    def view(ref, u, taken, digit, bit):
        left = [d for d in range(nd) if d not in taken]
        at = left.index(digit)
        return ref.at[tuple([slice(None)] * at + [bit])]

    def finish(u, step):
        flight[u, step].wait_recv()
        got = recv[u][step]
        if step == 0:
            got[...] = got[...] + acc0[u][...]
        else:
            taken = orders[u][:step]
            digit = orders[u][step]
            prev = recv[u][step - 1]
            own = view(prev, u, taken, digit, plan.mine(digit))
            got[...] = got[...] + own[...]

    def begin(u, step):
        taken = orders[u][:step]
        digit = orders[u][step]
        prev = recv[u][step - 1]
        src = view(prev, u, taken, digit, 1 - plan.mine(digit))
        flight[u, step] = send(u, step, src, recv[u][step], digit)

    def vstart(step):
        flight["v", step] = send(nu, step, vsum.at[step], vrecv.at[step], step)

    def vfinish(step):
        flight["v", step].wait_recv()
        vsum[step + 1] = vsum[step] + vrecv[step]

    me = plan.mine(core)
    for u in range(nu):
        s0 = send0[u]
        blocks(u, 1 - me, s0)
        if u == 0:
            pl.semaphore_wait(barrier, nd)
            if n_vec:
                vsum[0] = vec_ref[...]
                vstart(0)
        flight[u, 0] = send(u, 0, s0, recv[u][0], core)
        blocks(u, me, acc0[u])
        if u > 0:
            finish(u - 1, 0)
            begin(u - 1, 1)
    finish(nu - 1, 0)
    begin(nu - 1, 1)
    if n_vec:
        vfinish(0)
        vstart(1)
    for step in range(1, nd):
        for u in range(nu):
            finish(u, step)
            if step + 1 < nd:
                begin(u, step + 1)
            else:
                out_refs[u][...] = recv[u][step][...].astype(jnp.float32)
        if n_vec:
            vfinish(step)
            if step + 1 < nd:
                vstart(step + 1)
    if n_vec:
        vec_out[...] = vsum[nd]
    for copy in copies:
        copy.wait_send()


def wgrad_rs(plan, units, vec, cid, name):
    nd = len(plan.digits)
    core = bits_of(plan.n_frame) - 1
    ins, outs, bufs0, recvs = [], [], [], []
    flops = 0
    for unit in units:
        rows, height = unit["a"].shape
        width = unit["b"].shape[2]
        ins += [unit["a"], unit["b"]]
        flops += 2 * rows * height * width * plan.n_frame
        block = (width, height // plan.n_items) if unit["t"] else (height // plan.n_items, width)
        outs.append(jax.ShapeDtypeStruct(block, jnp.float32))
        bufs0.append(pltpu.VMEM((2,) * (nd - 1) + block, jnp.bfloat16))
        recvs += [pltpu.VMEM((2,) * (nd - 1 - s) + block, jnp.bfloat16) for s in range(nd)]
    scratch = bufs0 + bufs0 + recvs
    if vec is not None:
        ins.append(vec)
        outs.append(jax.ShapeDtypeStruct(vec.shape, jnp.float32))
        scratch += [pltpu.VMEM((nd + 1,) + vec.shape, jnp.float32), pltpu.VMEM((nd,) + vec.shape, jnp.float32)]
    count = len(units) + (vec is not None)
    scratch += [pltpu.SemaphoreType.DMA((count, nd))] * 2
    whole = pl.BlockSpec(memory_space=pltpu.VMEM)
    return pl.pallas_call(
        functools.partial(wgrad_kernel, plan, units_static(units), vec is not None),
        out_shape=outs, in_specs=[whole] * len(ins), out_specs=[whole] * len(outs),
        scratch_shapes=scratch,
        compiler_params=pltpu.CompilerParams(collective_id=cid, has_side_effects=True, vmem_limit_bytes=60 << 20),
        cost_estimate=pl.CostEstimate(flops=flops, bytes_accessed=40 << 20, transcendentals=0),
        name=name,
    )(*ins)


def units_static(units):
    return [{"t": unit["t"], "order": unit["order"]} for unit in units]


def code_table(width):
    first = width // 4
    other = (width - first) // 2

    def table(count, positions):
        half_count = count // 2
        frequency = 10000.0 ** (-np.arange(half_count, dtype=np.float64) / half_count)
        angles = np.arange(positions)[:, None] * frequency[None, :]
        return np.concatenate([np.sin(angles), np.cos(angles)], axis=1)

    out = np.zeros((128, width), np.float32)
    out[0:4, :first] = table(first, 4)
    out[32:64, first:first + other] = table(other, 32)
    out[64:64 + SIDE, first + other:] = table(other, SIDE)
    return out


def placement_code(frames, places, width):
    column = lax.broadcasted_iota(jnp.int32, (places.shape[0], 128), 1)
    hot = (column == frames[:, None]) | (column == 32 + (places // SIDE)[:, None]) | (column == 64 + (places % SIDE)[:, None])
    return jnp.dot(hot.astype(jnp.float32), jnp.asarray(code_table(width)), precision=lax.Precision.HIGHEST)


def norm_parts(x):
    centred = x - jnp.mean(x, axis=-1, keepdims=True)
    rstd = lax.rsqrt(jnp.mean(centred * centred, axis=-1, keepdims=True) + EPSILON)
    return centred * rstd, rstd


def norm_back(dn, hat, rstd, gain):
    g = dn * gain
    dx = rstd * (g - jnp.mean(g, axis=-1, keepdims=True) - hat * jnp.mean(g * hat, axis=-1, keepdims=True))
    return dx, jnp.sum(dn * hat, axis=0), jnp.sum(dn, axis=0)


def mm(a, b):
    return jnp.dot(a, b, preferred_element_type=jnp.float32)


def mm_t(a, b):
    return lax.dot_general(a, b, (((1,), (1,)), ((), ())), preferred_element_type=jnp.float32)


def total(x):
    return jnp.sum(x.astype(jnp.float32), axis=0)


def low(x):
    return x.astype(jnp.bfloat16)


def gelu_pair(hidden):
    cdf = 0.5 * (1.0 + lax.erf(hidden * np.float32(0.5 ** 0.5)))
    pdf = jnp.exp(-0.5 * hidden * hidden) * np.float32((2 * np.pi) ** -0.5)
    return hidden * cdf, cdf + hidden * pdf


def post_forward(carried, attended, params):
    (_, _, _, _, _, outward, outward_bias, second_gain, second_shift, expand, expand_bias, contract, contract_bias) = params
    mixed = carried + mm(attended, outward) + outward_bias
    hat, rstd = norm_parts(mixed)
    second = low(hat * second_gain + second_shift)
    hidden = mm(second, expand) + expand_bias
    act, slope = gelu_pair(hidden)
    activated = low(act)
    output = mixed + mm(activated, contract) + contract_bias
    return output, (hat, rstd, second, activated, slope)


def post_backward(gy, kept, params):
    (_, _, _, _, _, outward, _, second_gain, _, expand, _, contract, _) = params
    hat, rstd, second, activated, slope = kept
    dz = low(gy)
    du = low(mm_t(dz, contract) * slope)
    db = mm_t(du, expand)
    part, g_gain, g_shift = norm_back(db, hat, rstd, second_gain)
    dh = gy + part
    da = low(dh)
    do = low(mm_t(da, outward))
    vectors = dict(contract_bias=total(dz), expand_bias=total(du), outward_bias=total(da), second_gain=g_gain, second_shift=g_shift)
    return dh, da, do, du, dz, vectors


def by_frame(x, n_frame):
    rows, width = x.shape
    return x.reshape(rows, n_frame, width // n_frame).transpose(1, 0, 2)


NAMES = ("norm_gain", "norm_shift", "inward", "query_bias", "value_bias", "outward", "outward_bias", "second_gain", "second_shift", "expand", "expand_bias", "contract", "contract_bias")
MATRICES = ("inward", "outward", "expand", "contract")


def body(n_items, n_frame, tokens, visible_place, item_index, out_cotangent, *weights):
    enc_params, (embed_weight, embed_bias, mask_token), dec_params = weights[0:13], weights[13:16], weights[16:29]
    frame = lax.axis_index("frame")
    items_row = item_index[0]
    count, width = items_row.shape[0], mask_token.shape[0]
    vis, wide = tokens.shape
    depth_e, depth_d = wide // HEADS_E, width // HEADS_D
    long, short = count // 2, count // 4
    first_long = items_row[0] == items_row[long - 1]
    last_long = items_row[long] == items_row[count - 1]
    b0 = jnp.where(first_long, 0, jnp.where(last_long, long, short))
    b1 = jnp.where(first_long, long, 0)
    b2 = jnp.where(last_long, short, long + short)
    starts, sizes = (b0, b1, b2), (long, short, short)
    firsts = (0, long, long + short)

    def to_runs(x):
        return jnp.concatenate([lax.dynamic_slice_in_dim(x, s, n, 0) for s, n in zip(starts, sizes)], axis=0)

    def from_runs(x):
        out = jnp.zeros_like(x)
        for s, n, at in zip(starts, sizes, firsts):
            out = lax.dynamic_update_slice_in_dim(out, x[at:at + n], s, 0)
        return out

    end1, end2 = jnp.sum(items_row < 1), jnp.sum(items_row < 2)
    tokens_all = lax.all_gather(tokens, "frame", axis=0, tiled=True)
    places_all = lax.all_gather(visible_place, "frame", axis=0, tiled=True)
    flat = places_all.reshape(-1)
    ids_all = (flat >= end1).astype(jnp.int32) + (flat >= end2).astype(jnp.int32)
    ids_loc = lax.dynamic_slice_in_dim(ids_all, frame * vis, vis)
    frames_e = jnp.repeat(jnp.arange(n_frame, dtype=jnp.int32), vis)
    x0_all = tokens_all.astype(jnp.float32) + placement_code(frames_e, flat, wide)
    ehat_all, erstd_all = norm_parts(x0_all)
    (gain, shift, inward, qb, vb) = enc_params[:5]
    enormed_all = low(ehat_all * gain + shift)
    mine = lambda x: lax.dynamic_slice_in_dim(x, frame * vis, vis, 0)
    enormed = mine(enormed_all)
    ehat, erstd, x0 = mine(ehat_all), mine(erstd_all), mine(x0_all)
    eq = low(mm(enormed, inward[:, :wide]) + qb)
    ek = low(mm(enormed_all, inward[:, wide:2 * wide]))
    ev = low(mm(enormed_all, inward[:, 2 * wide:]) + vb)
    esegs = ((0, vis, 0, n_frame * vis),)
    qpad = -(-vis // LANE) * LANE
    eids = (jnp.broadcast_to(jnp.pad(ids_loc, (0, qpad - vis))[None, :], (8, qpad)), jnp.broadcast_to(ids_all[:, None], (n_frame * vis, LANE)))
    eo, else_ = attn_fwd(eq, ek, ev, depth_e, esegs, 1600, eids)
    enc_out, ekept = post_forward(x0, eo, enc_params)
    encoded = low(enc_out)

    encoded_all = lax.all_gather(encoded, "frame", axis=0, tiled=True)
    delta = mm(encoded_all, embed_weight) + embed_bias - mask_token
    high = low(delta)
    rest = low(delta - high.astype(jnp.float32))
    pair = jnp.concatenate([high.reshape(n_frame, vis, width), rest.reshape(n_frame, vis, width)], axis=1)
    local = jnp.arange(count, dtype=jnp.int32)
    place_runs = jnp.concatenate([s + jnp.arange(n, dtype=jnp.int32) for s, n in zip(starts, sizes)])
    table = jnp.asarray(code_table(width))[:n_frame]
    code = placement_code(jnp.full((count,), 127, jnp.int32), place_runs, width)
    hots, xs, masked = [], [], []
    for at, n in zip(firsts, sizes):
        hot = place_runs[at:at + n][None, :, None] == places_all[:, None, :]
        hots.append(low(hot))
        masked.append(1.0 - jnp.sum(hot.astype(jnp.float32), axis=2))
        picked = jnp.einsum("fpj,fjd->fpd", jnp.concatenate([hots[-1], hots[-1]], axis=2), pair, preferred_element_type=jnp.float32)
        xs.append((picked + mask_token + code[at:at + n][None] + table[:, None, :]).reshape(n_frame * n, width))
    xd_all = jnp.concatenate(xs, axis=0)
    masked_all = jnp.concatenate([m.reshape(-1) for m in masked])
    key_firsts = tuple(n_frame * at for at in firsts)

    def own(x):
        return jnp.concatenate([lax.dynamic_slice_in_dim(x, k + frame * n, n, 0) for k, n in zip(key_firsts, sizes)], axis=0)

    dhat_all, drstd_all = norm_parts(xd_all)
    (gain, shift, inward, qb, vb) = dec_params[:5]
    dnormed_all = low(dhat_all * gain + shift)
    dnormed, dhat, drstd, xd = own(dnormed_all), own(dhat_all), own(drstd_all), own(xd_all)
    dq_in = low(mm(dnormed, inward[:, :width]) + qb)
    dk_in = low(mm(dnormed_all, inward[:, width:2 * width]))
    dv_in = low(mm(dnormed_all, inward[:, 2 * width:]) + vb)
    dsegs = tuple((at, n, k, n_frame * n) for at, n, k in zip(firsts, sizes, key_firsts))
    do_out, dlse = attn_fwd(dq_in, dk_in, dv_in, depth_d, dsegs, 1600)
    dec_out, dkept = post_forward(xd, do_out, dec_params)
    decoded = from_runs(low(dec_out))

    gy = to_runs(out_cotangent).astype(jnp.float32)
    dh, da, do, du, dz, dvec = post_backward(gy, dkept, dec_params)
    gq, gk, gv = attn_bwd(dq_in, dk_in, dv_in, do, do_out, dlse, depth_d, dsegs, 1600)
    gkv = jnp.concatenate([gk, gv], axis=1)
    dn_q = mm_t(gq, inward[:, :width])
    dn_kv = mm_t(gkv, inward[:, width:])
    dx_q, g1, s1 = norm_back(dn_q, dhat, drstd, gain)
    dx_all, g2, s2 = norm_back(dn_kv, dhat_all, drstd_all, gain)
    dvec.update(norm_gain=g1 + g2, norm_shift=s1 + s2, query_bias=total(gq), value_bias=total(gv))
    dx_loc = dh + dx_q
    mask_grad = jnp.sum(dx_all * masked_all[:, None], axis=0) + jnp.sum(dx_loc * own(masked_all)[:, None], axis=0)
    low_all, low_loc = low(dx_all), low(dx_loc)
    de_part = 0.0
    de_loc = 0.0
    for hot, k, at, n in zip(hots, key_firsts, firsts, sizes):
        de_part = de_part + jnp.einsum("fpj,fpd->fjd", hot, low_all[k:k + n_frame * n].reshape(n_frame, n, width), preferred_element_type=jnp.float32)
        de_loc = de_loc + jnp.einsum("pj,pd->jd", lax.dynamic_index_in_dim(hot, frame, 0, keepdims=False), low_loc[at:at + n], preferred_element_type=jnp.float32)
    de_sum = lax.psum_scatter(low(de_part.reshape(n_frame * vis, width)), "frame", scatter_dimension=0, tiled=True)
    de = low(de_sum.astype(jnp.float32) + de_loc)
    own_rows = lax.broadcasted_iota(jnp.int32, (n_frame * count, 1), 0)
    zq = jnp.zeros((n_frame * count, width), jnp.bfloat16)
    for k, at, n in zip(key_firsts, firsts, sizes):
        zq = lax.dynamic_update_slice_in_dim(zq, gq[at:at + n], k + frame * n, 0)
    dproj_d = jnp.concatenate([zq, gkv], axis=1)

    dy = mm_t(de, embed_weight)
    eh, ea, eo_grad, eu, ez, evec = post_backward(dy, ekept, enc_params)
    hq, hk, hv = attn_bwd(eq, ek, ev, eo_grad, eo, else_, depth_e, esegs, 1600, eids)
    hkv = jnp.concatenate([hk, hv], axis=1)
    (gain, shift, inward, qb, vb) = enc_params[:5]
    en_q = mm_t(hq, inward[:, :wide])
    en_kv = mm_t(hkv, inward[:, wide:])
    ex_q, g1, s1 = norm_back(en_q, ehat, erstd, gain)
    ex_all, g2, s2 = norm_back(en_kv, ehat_all, erstd_all, gain)
    evec.update(norm_gain=g1 + g2, norm_shift=s1 + s2, query_bias=total(hq), value_bias=total(hv))
    ex_sum = lax.psum_scatter(low(ex_all), "frame", scatter_dimension=0, tiled=True)
    tokens_grad = eh + ex_q + ex_sum.astype(jnp.float32)
    zq = lax.dynamic_update_slice_in_dim(jnp.zeros((n_frame * vis, wide), jnp.bfloat16), hq, frame * vis, 0)
    dproj_e = jnp.concatenate([zq, hkv], axis=1)

    pairs = {
        ("e", "inward"): (enormed_all, dproj_e), ("e", "outward"): (eo, ea), ("e", "expand"): (ekept[2], eu), ("e", "contract"): (ekept[3], ez),
        ("m", "weight"): (encoded, de),
        ("d", "inward"): (dnormed_all, dproj_d), ("d", "outward"): (do_out, da), ("d", "expand"): (dkept[2], du), ("d", "contract"): (dkept[3], dz),
    }
    vectors = [evec[n] for n in NAMES if n not in MATRICES] + [total(de), mask_grad] + [dvec[n] for n in NAMES if n not in MATRICES]
    packed = jnp.concatenate([v.reshape(n_items, -1) for v in vectors], axis=1)
    tiles = all((a.shape[1] // n_items) % 16 == 0 for a, _ in pairs.values()) and n_frame == 4
    if tiles:
        plan = Plan(n_items, n_frame)
        y, x, z1 = 0, len(plan.digits) - 1, len(plan.digits) - 2
        upper = list(range(2, len(plan.digits) - 2))[::-1]
        orders = [[y, x, z1] + upper, [x, z1, y] + upper, [z1, y, x] + upper]
        unit = lambda key, order, t=False: dict(a=pairs[key][0], b=by_frame(pairs[key][1], n_frame), t=t, order=orders[order])
        keys_d = [("d", "contract"), ("d", "expand"), ("d", "outward"), ("m", "weight"), ("d", "inward")]
        got_d = wgrad_rs(plan, [unit(k, o) for k, o in zip(keys_d, (0, 1, 2, 0, 2))], None, 0, "decoder_weight_gradients")
        keys_e = [("e", "contract"), ("e", "expand"), ("e", "outward"), ("e", "inward")]
        turn = (pairs[keys_e[0]][0].shape[1] // n_items) % LANE == 0
        got_e = wgrad_rs(plan, [unit(k, o, t) for k, o, t in zip(keys_e, (0, 1, 2, 2), (turn, False, False, False))], packed, 1, "encoder_weight_gradients")
        grads = dict(zip(keys_d + keys_e, list(got_d) + list(got_e)))
        if turn:
            grads[keys_e[0]] = grads[keys_e[0]].T
        summed = got_e[-1]
    else:
        grads = {}
        for key, (a, b) in pairs.items():
            part = low(lax.dot_general(a, b, (((0,), (0,)), ((), ())), preferred_element_type=jnp.float32))
            part = lax.psum_scatter(part, "frame", scatter_dimension=1, tiled=True)
            grads[key] = lax.psum_scatter(part, "items", scatter_dimension=0, tiled=True).astype(jnp.float32)
        summed = lax.psum(packed, ("items", "frame"))
    row = lax.dynamic_index_in_dim(summed, lax.axis_index("items"), 0, keepdims=False)
    pieces, at = [], 0
    for v in vectors:
        n = v.shape[0] // n_items
        pieces.append(row[at:at + n])
        at += n
    pieces = iter(pieces)
    enc_grads = [grads["e", n] if n in MATRICES else next(pieces) for n in NAMES]
    mid_grads = [grads["m", "weight"], next(pieces), next(pieces)]
    dec_grads = [grads["d", n] if n in MATRICES else next(pieces) for n in NAMES]
    return (encoded, decoded, tokens_grad, *enc_grads, *mid_grads, *dec_grads)


def solution(mesh):
    rows = P(("items", "frame"), None)
    block = [P("items", "frame") if n in MATRICES else P("items") for n in NAMES]
    return jax.shard_map(
        functools.partial(body, mesh.shape["items"], mesh.shape["frame"]),
        mesh=mesh,
        in_specs=(rows,) * 4 + (P(),) * 29,
        out_specs=(rows,) * 3 + tuple(block) + (P("items", "frame"), P("items"), P("items")) + tuple(block),
        check_vma=False,
    )
```

time: 2670 us -> 535 us (0.20)
  waiting for transfers between devices: 1250 us -> 17.9 us
  matrix products: 775 us -> 75 us
  Pallas kernels: 0 us -> 266 us
  other arithmetic: 261 us -> 42.8 us
  local copies, waits for them, and re-layouts: 222 us -> 99.9 us
  loops' own time: 92 us -> 0 us
    reduce_scatter x11 -> x2, waiting for transfers between devices: 908 us -> 0.04 us  [the longest x1 0.02 us: body(): lax.psum_scatter(low(de_part.reshape(n_frame * vis, width)), 'frame', sca...]
    dot_general x223 -> x35, matrix products: 775 us -> 75 us  [the longest x11 38.2 us: mm_t(): lax.dot_general(a, b, (((1,), (1,)), ((), ())), preferred_element_type=jn...]
    unnamed x39 -> x4, waiting for transfers between devices: 277 us -> 0.73 us
    pallas_call x0 -> x6, Pallas kernels: none -> 266 us  [the longest x2 153 us: wgrad_rs(): pl.pallas_call(functools.partial(wgrad_kernel, plan, units_static(units),...]
    convert_element_type x51 -> x5, other arithmetic: 204 us -> 9.25 us  [low(): return x.astype(jnp.bfloat16)]
    another operation x4 -> x0, loops' own time: 92 us -> none  [the longest x2 73.5 us: attention_backward(): lax.map(one_head, jnp.arange(head_count, dtype=jnp.int32))]
    dynamic_slice x84 -> x9, local copies, waits for them, and re-layouts: 71.7 us -> 7.8 us  [the longest x7 6.66 us: own(): lax.dynamic_slice_in_dim(x, k + frame * n, n, 0)]
    unnamed x241 -> x234, local copies, waits for them, and re-layouts: 82.1 us -> 20.2 us
  transfers between devices with their start and end apart: 27 -> 4, of which waited for: 24 -> 2; matrix products, arithmetic and copies ran while one was open for 7% -> 18% of each run, Pallas kernels for 0% -> 29%
where the time goes in v1:
time: 535 us; the launch traced here: 527 us
  Pallas kernels  266 us (50%)
  local copies, waits for them, and re-layouts  99.9 us (19%)
  matrix products  75 us (14%)
  other arithmetic  42.8 us (8%)
  between operations  18.3 us (3%)
  waiting for transfers between devices  17.9 us (3%)
  blocking collectives  6.28 us (1%)
    pallas_call x2, Pallas kernels, wgrad_rs(): pl.pallas_call(functools.partial(wgrad_kernel, plan, units_static(units),...  153 us
    pallas_call x2, Pallas kernels, attn_bwd(): pl.pallas_call(functools.partial(bwd_kernel, depth, segs, kc, ids is not...  67.8 us
    pallas_call x2, Pallas kernels, attn_fwd(): pl.pallas_call(functools.partial(fwd_kernel, depth, segs, kc, ids is not...  46 us
    dot_general x11, matrix products, mm_t(): lax.dot_general(a, b, (((1,), (1,)), ((), ())), preferred_element_type=jn...  38.2 us
    reshape x9, local copies, waits for them, and re-layouts, by_frame(): return x.reshape(rows, n_frame, width // n_frame).transpose(1, 0, 2)  31.1 us
    dot_general x13, matrix products, mm(): return jnp.dot(a, b, preferred_element_type=jnp.float32)  22 us
    unnamed x234, local copies, waits for them, and re-layouts  20.2 us
    concatenate x1, local copies, waits for them, and re-layouts, body(): dproj_d = jnp.concatenate([zq, gkv], axis=1)  13.1 us
  transfers between devices with their start and end apart: 4, of which 2 were waited for; matrix products, arithmetic and copies ran while one was open for 18% of the time, Pallas kernels for 29%

profile of v1, /device:TPU:0, one launch (start us, length us, event | category | flops | bytes accessed | tf_op | source)
XLA Modules:
  0.0 526.8 jit_solution(3173205720729538067)
XLA Ops:
  8.0 6.3 %all-gather = s32[4,1,200]{2,1,0:T(1,128)S(1)} all-gather(s32[1,1,200]{2,1,0:T(1,128)} %bitcast.200), channel_id=1, replica_groups=mesh['items'=8,'frame'=4] {'frame'}, dimensions={0}, use_global_device_ids=true | all-gather | bytes 4000 | tf_op jit(solution)/shard_map/all_gather | solution.py:456
  21.6 8.5 %all-gather.4.cloned.1.call-done = bf16[800,768]{1,0:T(8,128)(2,1)} async-done(((bf16[200,768]{1,0:T(8,128)(2,1)}), bf16[800,768]{1,0:T(8,128)(2,1)}) %all-gather.4.cloned.1.call-update) | async-done | bytes 1228816 | tf_op jit(solution)/shard_map/all_gather | solution.py:455
  39.6 9.1 %attention_forward.2 = (bf16[200,768]{1,0:T(8,128)(2,1)S(1)}, f32[6,1,8,256]{3,2,1,0:T(8,128)S(1)}) custom-call(bf16[200,768]{1,0:T(8,128)(2,1)S(1)} %fusion.42.refs_0_, bf16[800,768]{1,0:T(8,128)(2,1)S(1)} %convolution_convert_fusion.1.refs_1_, bf16[800,768]{1,0:T(8,128)(2,1)S(1)} %add_convert_fusion.1.refs_2_, ...), custom_call_target="tpu_custom_call" | custom-call | flops 491520000 | bytes 3072000 | tf_op jit(solution)/shard_map/attention_forward/pallas_call | solution.py:77
  64.9 8.5 %all-gather.6.cloned.1.call-done = bf16[800,768]{1,0:T(8,128)(2,1)} async-done(((bf16[200,768]{1,0:T(8,128)(2,1)}), bf16[800,768]{1,0:T(8,128)(2,1)}) %all-gather.6.cloned.1.call-update) | async-done | bytes 1228816 | tf_op jit(solution)/shard_map/all_gather | solution.py:478
  82.6 5.3 %add_convert_fusion = (bf16[3200,512]{1,0:T(8,128)(2,1)S(1)}, f32[3200,512]{1,0:T(8,128)S(1)}, f32[3200,512]{1,0:T(8,128)}) fusion(f32[512]{0:T(512)S(1)} %copy-done.87, f32[512]{0:T(512)S(1)} %copy-done.64, f32[3200]{0:T(1024)S(1)} %add_rsqrt_fusion, f32[3200]{0:T(1024)S(1)} %broadcast_multiply_fusion.2, f32[800,512]{1,0:T(8,128)S(1)} %bitcast.168, ...), kind=kLoop, calls=%fused_computation.22 | loop fusion | flops 11468800 | bytes 22967296 | tf_op jit(solution)/shard_map/convert_element_type | solution.py:385
  88.0 3.2 constant_dynamic-slice_fusion.11
  96.6 3.6 fusion.10.refs_2_
  100.9 36.8 %attention_forward.3 = (bf16[800,512]{1,0:T(8,128)(2,1)S(1)}, f32[4,3,8,512]{3,2,1,0:T(8,128)S(1)}) custom-call(bf16[800,512]{1,0:T(8,128)(2,1)S(1)} %add_convert_fusion.6.refs_0_, bf16[3200,512]{1,0:T(8,128)(2,1)S(1)} %convolution_convert_fusion.refs_1_, bf16[3200,512]{1,0:T(8,128)(2,1)} %fusion.10.refs_2_), custom_call_target="tpu_custom_call" | custom-call | flops 1966080000 | bytes 8192000 | tf_op jit(solution)/shard_map/attention_forward/pallas_call | solution.py:77
  139.2 3.3 multiply_convert_fusion
  147.3 5.3 %convert_reduce_fusion = (f32[2048]{0:T(1024)S(1)}, bf16[800,2048]{1,0:T(8,128)(2,1)S(1)}) fusion(f32[800,2048]{1,0:T(8,128)S(1)} %get-tuple-element.176, f32[2048]{0:T(1024)S(1)} %copy-done.92, bf16[2048,512]{1,0:T(8,128)(2,1)S(1)} %copy-done.90, bf16[200,512]{1,0:T(8,128)(2,1)S(1)} %get-tuple-element.131, bf16[200,512]{1,0:T(8,128)(2,1)S(1)} %get-tuple-element.130, ...), kind=kOutput, calls=%fused_computation.14 | convolution fusion | flops 1701476352 | bytes 12763136 | tf_op jit(solution)/shard_map/dot_general | solution.py:377
  158.0 56.7 %attention_backward.2 = (bf16[800,512]{1,0:T(8,128)(2,1)S(1)}, bf16[3200,512]{1,0:T(8,128)(2,1)}, bf16[3200,512]{1,0:T(8,128)(2,1)}) custom-call(bf16[800,512]{1,0:T(8,128)(2,1)S(1)} %add_convert_fusion.6.refs_0_, bf16[3200,512]{1,0:T(8,128)(2,1)} %copy-done.10, bf16[3200,512]{1,0:T(8,128)(2,1)} %fusion.10.refs_2_, ...), custom_call_target="tpu_custom_call" | custom-call | flops 4915200000 | bytes 16384000 | tf_op jit(solution)/shard_map/attention_backward/pallas_call | solution.py:140
  214.7 7.9 %multiply_reduce_fusion = (f32[512]{0:T(512)S(1)}, f32[3200]{0:T(1024)S(1)}, f32[3200]{0:T(1024)S(1)}, f32[512]{0:T(512)S(1)}, f32[3200,512]{1,0:T(8,128)S(1)}) fusion(f32[3200,512]{1,0:T(8,128)S(1)} %bitcast.161, f32[512]{0:T(512)S(1)} %copy-done.64, bf16[512,1536]{1,0:T(8,128)(2,1)} %param.58, bf16[3200,512]{1,0:T(8,128)(2,1)} %get-tuple-element.56, ...), kind=kOutput, calls=%fused_computation.16 | convolution fusion | flops 3380012032 | bytes 20741120 | tf_op jit(solution)/shard_map/dot_general | solution.py:377
  234.6 6.4 %pad_maximum_fusion = bf16[3200,1536]{1,0:T(8,128)(2,1)} fusion(bf16[3200,512]{1,0:T(8,128)(2,1)S(1)} %copy-done.12, bf16[3200,512]{1,0:T(8,128)(2,1)} %get-tuple-element.55, bf16[3200,512]{1,0:T(8,128)(2,1)S(1)} %slice_dynamic-update-slice_fusion.4), kind=kLoop, calls=%fused_computation | loop fusion | flops 29491200 | bytes 19660800 | tf_op jit(solution)/shard_map/concatenate | solution.py:536
  251.8 4.0 copy.127
  256.9 13.1 %copy.100 = bf16[3200,1536]{0,1:T(8,128)(2,1)} copy(bf16[3200,1536]{1,0:T(8,128)(2,1)} %pad_maximum_fusion) | data formatting | bytes 19660800 | tf_op jit(solution)/shard_map/concatenate | solution.py:536
  270.0 13.9 %copy.101 = bf16[3200,4,384]{2,0,1:T(8,128)(2,1)} copy(bf16[3200,4,384]{0,2,1:T(8,128)(2,1)} %bitcast.159) | data formatting | bytes 19660800 | tf_op jit(solution)/shard_map/reshape | solution.py:422
  294.0 6.7 %convert_reduce_fusion.2 = (f32[3072]{0:T(1024)}, bf16[200,3072]{1,0:T(8,128)(2,1)S(1)}) fusion(f32[200,3072]{1,0:T(8,128)} %get-tuple-element.172, bf16[200,768]{1,0:T(8,128)(2,1)S(1)} %get-tuple-element.107, bf16[3072,768]{1,0:T(8,128)(2,1)} %param.51), kind=kOutput, calls=%fused_computation.47 | convolution fusion | flops 951088128 | bytes 8724480 | tf_op jit(solution)/shard_map/dot_general | solution.py:377
  309.7 11.2 %attention_backward.3 = (bf16[200,768]{1,0:T(8,128)(2,1)S(1)}, bf16[800,768]{1,0:T(8,128)(2,1)S(1)}, bf16[800,768]{1,0:T(8,128)(2,1)S(1)}) custom-call(bf16[200,768]{1,0:T(8,128)(2,1)S(1)} %copy-done.9, bf16[800,768]{1,0:T(8,128)(2,1)S(1)} %copy-done.5, bf16[800,768]{1,0:T(8,128)(2,1)} %copy-done.6, bf16[200,768]{1,0:T(8,128)(2,1)S(1)} %convolution_convert_fusion.3.refs_3_, ...), custom_call_target="tpu_custom_call" | custom-call | flops 1228800000 | bytes 6144000 | tf_op jit(solution)/shard_map/attention_backward/pallas_call | solution.py:140
  320.9 4.1 multiply_reduce_fusion.5
  326.6 3.0 multiply_reduce_fusion.18
  334.5 6.2 %copy.94 = bf16[800,2304]{0,1:T(8,128)(2,1)} copy(bf16[800,2304]{1,0:T(8,128)(2,1)} %pad_maximum_fusion.2) | data formatting | bytes 7372800 | tf_op jit(solution)/shard_map/concatenate | solution.py:551
  340.8 7.1 %copy.95 = bf16[800,4,576]{2,0,1:T(8,128)(2,1)} copy(bf16[800,4,576]{0,2,1:T(8,128)(2,1)} %bitcast.165) | data formatting | bytes 7372800 | tf_op jit(solution)/shard_map/reshape | solution.py:422
  349.7 95.8 %encoder_weight_gradients.1 = (f32[192,384]{1,0:T(8,128)}, f32[96,768]{1,0:T(8,128)}, f32[96,192]{1,0:T(8,128)}, f32[96,576]{1,0:T(8,128)}, f32[8,2048]{1,0:T(8,128)}) custom-call(bf16[200,3072]{1,0:T(8,128)(2,1)} %copy-done.38, bf16[4,200,192]{2,1,0:T(8,128)(2,1)} %bitcast.187, bf16[200,768]{1,0:T(8,128)(2,1)} %copy-done.36, ...), custom_call_target="tpu_custom_call" | custom-call | flops 4954521600 | bytes 41943040 | tf_op jit(solution)/shard_map/encoder_weight_gradients/pallas_call | solution.py:323
  446.3 56.7 %decoder_weight_gradients.1 = (f32[256,128]{1,0:T(8,128)}, f32[64,512]{1,0:T(8,128)}, f32[64,128]{1,0:T(8,128)}, f32[96,128]{1,0:T(8,128)}, f32[64,384]{1,0:T(8,128)}) custom-call(bf16[800,2048]{1,0:T(8,128)(2,1)} %copy-done.103, bf16[4,800,128]{2,1,0:T(8,128)(2,1)} %bitcast_bitcast_fusion.3.refs_1_, bf16[800,512]{1,0:T(8,128)(2,1)} %copy-done.42, ...), custom_call_target="tpu_custom_call" | custom-call | flops 8965324800 | bytes 41943040 | tf_op jit(solution)/shard_map/decoder_weight_gradients/pallas_call | solution.py:323
  (411 shorter events, 125.6 us)
Async XLA Ops:
  7.2 132.0 %copy-start = (bf16[512,2048]{1,0:T(8,128)(2,1)S(1)}, bf16[512,2048]{1,0:T(8,128)(2,1)}, u32[]{:S(2)}) copy-start(bf16[512,2048]{1,0:T(8,128)(2,1)} %param.65) | copy-start | bytes 6291460
  7.2 22.9 %all-gather.4.cloned.1.call-start = ((), (), s32[]{:S(2)}) async-start(), calls=%async_computation.2 | async-start | bytes 1536000 | tf_op jit(solution)/shard_map/all_gather | solution.py:455
  8.0 65.5 %all-gather.6.cloned.1.call-start = ((), (), s32[]{:S(2)}) async-start(), calls=%async_computation.3 | async-start | bytes 1536000 | tf_op jit(solution)/shard_map/all_gather | solution.py:478
  55.6 233.2 %reduce-scatter.3.cloned.1.call-start = ((), (), s32[]{:S(2)}) async-start(), calls=%async_computation.4 | async-start | bytes 1024000 | tf_op jit(solution)/shard_map/reduce_scatter | solution.py:530
  57.9 15.6 %copy-start.96 = (f32[512]{0:T(512)S(1)}, f32[512]{0:T(512)}, u32[]{:S(2)}) copy-start(f32[512]{0:T(512)} %param.54) | copy-start | bytes 6148
  57.9 15.6 %copy-start.97 = (f32[512]{0:T(512)S(1)}, f32[512]{0:T(512)}, u32[]{:S(2)}) copy-start(f32[512]{0:T(512)} %param.55) | copy-start | bytes 6148
  61.2 14.7 %copy-start.53 = (pred[4,200,200]{2,1,0:T(8,128)(4,1)}, pred[4,200,200]{2,1,0:T(8,128)(4,1)S(1)}, u32[]{:S(2)}) copy-start(pred[4,200,200]{2,1,0:T(8,128)(4,1)S(1)} %get-tuple-element.155) | copy-start | bytes 480004
  94.5 131.2 %copy-start.29 = (f32[200,512]{1,0:T(8,128)}, f32[200,512]{1,0:T(8,128)S(1)}, u32[]{:S(2)}) copy-start(f32[200,512]{1,0:T(8,128)S(1)} %get-tuple-element.117) | copy-start | bytes 1228804
  94.6 131.2 %copy-start.21 = (f32[400,512]{1,0:T(8,128)}, f32[400,512]{1,0:T(8,128)S(1)}, u32[]{:S(2)}) copy-start(f32[400,512]{1,0:T(8,128)S(1)} %constant_dynamic-slice_fusion.3) | copy-start | bytes 2457604
  100.8 36.9 %copy-start.45 = (f32[400,512]{1,0:T(8,128)S(1)}, f32[400,512]{1,0:T(8,128)}, u32[]{:S(2)}) copy-start(f32[400,512]{1,0:T(8,128)} %constant_dynamic-slice_fusion.12) | copy-start | bytes 2457604
  100.8 36.9 %copy-start.49 = (bf16[512,512]{1,0:T(8,128)(2,1)S(1)}, bf16[512,512]{1,0:T(8,128)(2,1)}, u32[]{:S(2)}) copy-start(bf16[512,512]{1,0:T(8,128)(2,1)} %param.61) | copy-start | bytes 1572868
  100.8 36.9 %copy-start.50 = (f32[200,512]{1,0:T(8,128)S(1)}, f32[200,512]{1,0:T(8,128)}, u32[]{:S(2)}) copy-start(f32[200,512]{1,0:T(8,128)} %get-tuple-element.121) | copy-start | bytes 1228804
  100.8 36.9 %copy-start.100 = (f32[512]{0:T(512)S(1)}, f32[512]{0:T(512)}, u32[]{:S(2)}) copy-start(f32[512]{0:T(512)} %param.62) | copy-start | bytes 6148
  137.7 20.3 %copy-start.7 = (bf16[800,512]{1,0:T(8,128)(2,1)}, bf16[800,512]{1,0:T(8,128)(2,1)S(1)}, u32[]{:S(2)}) copy-start(bf16[800,512]{1,0:T(8,128)(2,1)S(1)} %get-tuple-element.53.refs_4_) | copy-start | bytes 2457604
  157.4 57.3 %slice-start = ((s8[6553600]{0:T(1024)(128)(4,1)}), s8[4194304]{0:T(1024)(128)(4,1)S(1)}, s32[]{:S(2)}) async-start(s8[6553600]{0:T(1024)(128)(4,1)} %bitcast.160), calls=%async_computation.6 | async-start | bytes 8388608
  158.0 56.7 %slice-start.1 = ((s8[6553600]{0:T(1024)(128)(4,1)}), s8[2359296]{0:T(1024)(128)(4,1)S(1)}, s32[]{:S(2)}) async-start(s8[6553600]{0:T(1024)(128)(4,1)} %bitcast.160), calls=%async_computation.7 | async-start | bytes 4718592
  232.6 276.1 %reduce-scatter.5.cloned.1.call-start = ((), (), s32[]{:S(2)}) async-start(), calls=%async_computation.5 | async-start | bytes 1536000 | tf_op jit(solution)/shard_map/reduce_scatter | solution.py:548
  270.0 15.0 %copy-start.44 = (bf16[800,512]{1,0:T(8,128)(2,1)S(1)}, bf16[800,512]{1,0:T(8,128)(2,1)}, u32[]{:S(2)}) copy-start(bf16[800,512]{1,0:T(8,128)(2,1)} %copy-done.43) | copy-start | bytes 2457604
  305.3 15.5 %copy-start.62 = (f32[768]{0:T(1024)S(1)}, f32[768]{0:T(1024)}, u32[]{:S(2)}) copy-start(f32[768]{0:T(1024)} %param.40) | copy-start | bytes 9220
  349.7 95.8 %copy-start.28 = (bf16[200,512]{1,0:T(8,128)(2,1)S(1)}, bf16[200,512]{1,0:T(8,128)(2,1)}, u32[]{:S(2)}) copy-start(bf16[200,512]{1,0:T(8,128)(2,1)} %copy-done.27) | copy-start | bytes 614404
  446.3 62.4 %copy-start.26 = (f32[200,768]{1,0:T(8,128)S(1)}, f32[200,768]{1,0:T(8,128)}, u32[]{:S(2)}) copy-start(f32[200,768]{1,0:T(8,128)} %get-tuple-element.110) | copy-start | bytes 1843204
  446.3 62.4 %copy-start.48 = (f32[200,768]{1,0:T(8,128)S(1)}, f32[200,768]{1,0:T(8,128)}, u32[]{:S(2)}) copy-start(f32[200,768]{1,0:T(8,128)} %get-tuple-element.183) | copy-start | bytes 1843204
  446.3 62.4 %copy-start.81 = (f32[200]{0:T(256)S(1)}, f32[200]{0:T(256)}, u32[]{:S(2)}) copy-start(f32[200]{0:T(256)} %dynamic-slice.15) | copy-start | bytes 2404
  503.0 14.4 %copy-start.59 = (f32[64,384]{1,0:T(8,128)S(1)}, f32[64,384]{1,0:T(8,128)}, u32[]{:S(2)}) copy-start(f32[64,384]{1,0:T(8,128)} %get-tuple-element.252) | copy-start | bytes 294916
  (93 other events, 480.5 us)
Sparse Core Ops, SparseCore 0:
  9.6 20.4 all-gather.3
  55.7 17.7 all-gather.5
  232.7 23.4 reduce-scatter.2
  326.7 25.9 reduce-scatter.4
